TPU v7x, 512 devices: a whole 4x8x8 slice. The times are simulated.
512 devices in a mesh: pitch: 32 (over x, z), span: 8 (over y), row: 2 (over core).
Axes of the slice: x: 4, y: 8, z: 8, core: 2. Of those that a mesh axis runs over, the one named last changes fastest.
Arguments:
- fields: float32 [3, 512, 128, 512], P(None, 'pitch', 'span', 'row'), may hold values from -6 to 6
- diffusivity: float32 [512, 128, 512], P('pitch', 'span', 'row'), may hold values from 0.01 to 0.1
- mean_flow: bfloat16 [128, 2, 512], P('span', None, 'row'), may hold values from -6 to 6
- radial_kernel: bfloat16 [128, 128], replicated
- tracer_values: float32 [10, 1048576], P(None, ('pitch', 'span', 'row')), may hold values from -6 to 6
- tracer_cells: int32 [1048576], P(('pitch', 'span', 'row')), may hold values from 0 to 65535
- tracer_dest: int32 [1048576, 1], P(('pitch', 'span', 'row')), may hold values from 0 to 31; in each aligned block of 2048 rows (0 to 2047, 2048 to 4095, ...) at most 128 rows name the same one
- interface_map: int32 [2, 512], P('row', 'pitch'), may hold values from 0 to 511, as said below
Outputs:
- advected: float32 [3, 512, 128, 512], P(None, 'pitch', 'span', 'row')
- arrived: float32 [10, 2097152], P(None, ('pitch', 'span', 'row'))
Inputs may be any that keep to these rules, and one draw needn't show every extreme that they name: `tracer_cells`: the local index of the owning cell within the block of the device that holds the tracer, i * 16 * 256 + r * 256 + a for local indices i, r, a. `tracer_dest`: at most 128 of the tracers of one device go to one pitch index. `interface_map`: for one offset o of each draw, row 0 holds (i + o) mod 512 and row 1 holds (i - o) mod 512, so the two rows are inverse permutations.
All inputs are finite; a program needn't handle non-finite values.
Results may differ from a plain program's by a relative error of at most 0.0015.
Values may be sent and summed in bfloat16 or wider, within the bound.
A program may use at most 128 MiB of HBM per device.

v0:
```python
import jax
import jax.numpy as jnp
from jax import lax
from jax.sharding import PartitionSpec as P

SUB = 2
TIME_STEP = 0.9
AXIAL_SPEED = 0.15
PITCH_SPEED = 0.15


def swapped(block, axis, apart):
    count = lax.axis_size(axis)
    route = []
    for low in range(count):
        high = low | 1 << apart
        if high != low and high < count:
            route += [(low, high), (high, low)]
    return lax.ppermute(block, axis, route)


def padded(cells, sides, width):
    for axis, dim in sides:
        count = lax.axis_size(axis)
        head = lax.slice_in_dim(cells, 0, width, axis=dim)
        tail = lax.slice_in_dim(cells, cells.shape[dim] - width, cells.shape[dim], axis=dim)
        cells = jnp.concatenate(
            [
                lax.ppermute(tail, axis, [(i, (i + 1) % count) for i in range(count)]),
                cells,
                lax.ppermute(head, axis, [((i + 1) % count, i) for i in range(count)]),
            ],
            axis=dim,
        )
    return cells


def face_flux(left_values, right_values, left_kappa, right_kappa, face_speed):
    diffusion = -0.5 * (left_kappa + right_kappa) * (right_values - left_values)
    if face_speed is None:
        return diffusion
    return (
        jnp.maximum(face_speed, 0.0) * left_values
        + jnp.minimum(face_speed, 0.0) * right_values
        + diffusion
    )


def interface_ghost(own_face, local_map):
    across = swapped(own_face, "row", 0)
    picked = lax.all_gather(across, "pitch", axis=1, tiled=True)
    return jnp.take(picked, local_map, axis=1)


def update_core(extended, speed_axial, speed_pitch, ghost_face, wall_mask, row_id):
    along_pitch = extended[:, :, 1:-1, :]
    pitch_flux = face_flux(
        along_pitch[:3, :-1],
        along_pitch[:3, 1:],
        along_pitch[3, :-1],
        along_pitch[3, 1:],
        speed_pitch,
    )
    along_radius = extended[:, 1:-1]
    radial_flux = (
        face_flux(
            along_radius[:3, :, :-1],
            along_radius[:3, :, 1:],
            along_radius[3, :, :-1],
            along_radius[3, :, 1:],
            None,
        )
        * wall_mask[:, None]
    )
    core = extended[:, 1:-1, 1:-1]
    pitch_cells = core.shape[1]
    full_stack = jnp.concatenate(
        [core, jnp.broadcast_to(speed_axial[None, None], (1, pitch_cells) + speed_axial.shape)], 0
    )
    upstream = jnp.where(row_id == 0, full_stack[..., 0], ghost_face)
    downstream = jnp.where(row_id == 0, ghost_face, full_stack[..., -1])
    line = jnp.concatenate([upstream[..., None], full_stack, downstream[..., None]], -1)
    face_speed = 0.5 * (line[4, ..., :-1] + line[4, ..., 1:])
    axial_flux = face_flux(
        line[:3, ..., :-1], line[:3, ..., 1:], line[3, ..., :-1], line[3, ..., 1:], face_speed
    )
    divergence = (
        pitch_flux[:, 1:]
        - pitch_flux[:, :-1]
        + radial_flux[:, :, 1:]
        - radial_flux[:, :, :-1]
        + axial_flux[..., 1:]
        - axial_flux[..., :-1]
    )
    return core[:3] - TIME_STEP * divergence


def advance(state, diffusivity, speed_axial, speed_pitch, local_map, wall_mask):
    pitch_cells = state.shape[1]
    stacked = jnp.concatenate([state, diffusivity[None]], 0)
    extended = padded(stacked, (("pitch", 1), ("span", 2)), 1)
    full_stack = jnp.concatenate(
        [stacked, jnp.broadcast_to(speed_axial[None, None], (1, pitch_cells) + speed_axial.shape)],
        0,
    )
    row_id = lax.axis_index("row")
    own_face = jnp.where(row_id == 0, full_stack[..., -1], full_stack[..., 0])
    ghost_face = interface_ghost(own_face, local_map)
    return update_core(extended, speed_axial, speed_pitch, ghost_face, wall_mask, row_id)


def local(
    fields,
    diffusivity,
    mean_flow,
    radial_kernel,
    tracer_values,
    tracer_cells,
    tracer_dest,
    interface_map,
):
    radial_cells = mean_flow.shape[0]
    axial_cells = mean_flow.shape[2]
    flat_width = 2 * axial_cells
    span_id = lax.axis_index("span")
    kernel_cols = lax.dynamic_slice_in_dim(radial_kernel, span_id * radial_cells, radial_cells, 1)
    flat_rows = mean_flow.reshape(radial_cells, flat_width)
    smoothed = lax.psum_scatter(
        jnp.dot(kernel_cols, flat_rows, preferred_element_type=jnp.float32),
        "span",
        scatter_dimension=0,
        tiled=True,
    )
    smoothed = smoothed.reshape(radial_cells, 2, axial_cells)
    speed_axial = AXIAL_SPEED * (1.0 + 0.5 * jnp.tanh(smoothed[:, 0]))
    speed_pitch = PITCH_SPEED * jnp.tanh(smoothed[:, 1])
    plane_size = radial_cells * axial_cells
    sample_fields = jnp.take(fields.reshape(fields.shape[0], -1), tracer_cells, axis=1)
    sample_speed = jnp.take(
        jnp.stack([speed_axial, speed_pitch]).reshape(2, plane_size),
        tracer_cells % plane_size,
        axis=1,
    )
    sampled = jnp.concatenate([sample_fields, sample_speed], 0)
    head_rows = tracer_values[:5]
    tail_rows = tracer_values[5:]
    updated = jnp.concatenate(
        [head_rows + 0.5 * (sampled - head_rows), tail_rows + 0.8 * sampled], 0
    )
    npitch = lax.axis_size("pitch")
    capacity = 2 * tracer_values.shape[1] // npitch
    targets = tracer_dest[:, 0]
    onehot = (targets[:, None] == jnp.arange(npitch, dtype=jnp.int32)[None]).astype(jnp.int32)
    slot_index = jnp.sum((jnp.cumsum(onehot, 0) - onehot) * onehot, 1)
    position = targets * capacity + slot_index
    outgoing = (
        jnp.zeros((tracer_values.shape[0], npitch * capacity), jnp.float32)
        .at[:, position]
        .set(updated)
    )
    arrived = lax.all_to_all(outgoing, "pitch", split_axis=1, concat_axis=1, tiled=True)
    face_index = span_id * radial_cells + jnp.arange(radial_cells + 1, dtype=jnp.int32)
    total_radial = radial_cells * lax.axis_size("span")
    wall_mask = ((face_index > 0) & (face_index < total_radial)).astype(jnp.float32)
    local_map = interface_map[0]
    current = fields
    for substep in range(SUB):
        current = advance(current, diffusivity, speed_axial, speed_pitch, local_map, wall_mask)
    return (current, arrived)


def solution(mesh):
    placed = (
        P(None, "pitch", "span", "row"),
        P("pitch", "span", "row"),
        P("span", None, "row"),
        P(),
        P(None, ("pitch", "span", "row")),
        P(("pitch", "span", "row")),
        P(("pitch", "span", "row"), None),
        P("row", "pitch"),
    )
    return jax.shard_map(
        local,
        mesh=mesh,
        in_specs=placed,
        out_specs=(P(None, "pitch", "span", "row"), P(None, ("pitch", "span", "row"))),
        check_vma=False,
    )
```

profile of v0, /device:TPU:24, one launch (start us, length us, event | category | flops | bytes accessed | tf_op | source)
XLA Modules:
  0.0 287.4 jit_solution(10924218289385498217)
XLA Ops:
  7.2 1.1 copy.928
  8.4 1.3 constant_dynamic-update-slice_fusion
  9.8 0.7 fusion.65
  10.5 4.3 %collective-permute-start = (f32[4,1,16,256]{3,2,1,0:T(8,128)}, f32[4,1,16,256]{3,2,1,0:T(8,128)S(1)}, u32[]{:S(2)}, u32[]{:S(2)}) collective-permute-start(f32[4,1,16,256]{3,2,1,0:T(8,128)} %get-tuple-element.57), channel_id=1, source_target_pairs={{0,16},{16,32},{32,48},{48,64},{64,80},{80,96},{96,112},{112,128},... | collective-permute-start | bytes 196616 | tf_op jit(solution)/shard_map/ppermute | solution.py:29
  14.7 10.8 %collective-permute-start.1 = (f32[4,1,16,256]{3,2,1,0:T(8,128)}, f32[4,1,16,256]{3,2,1,0:T(8,128)}, u32[]{:S(2)}, u32[]{:S(2)}) collective-permute-start(f32[4,1,16,256]{3,2,1,0:T(8,128)} %get-tuple-element.58), channel_id=1, source_target_pairs={{16,0},{32,16},{48,32},{64,48},{80,64},{96,80},{112,96},{128,112},... | collective-permute-start | bytes 196616 | tf_op jit(solution)/shard_map/ppermute | solution.py:31
  25.6 0.9 fusion.48
  27.0 0.7 compare_and_fusion.2
  27.7 16.7 %copy.818 = f32[3,16,16,256]{0,3,2,1:T(8,128)} copy(f32[3,16,16,256]{3,2,1,0:T(8,128)S(1)} %copy-done.2) | data formatting | bytes 1572864 | tf_op args[0]
  44.4 18.2 %gather_fusion = f32[2048,3]{1,0:T(8,128)} fusion(f32[3,65536]{0,1:T(8,128)} %bitcast.121, s32[2048]{0:T(1024)S(1)} %get-tuple-element.74), kind=kCustom, calls=%fused_computation.2 | custom fusion | bytes 57344 | tf_op jit(solution)/shard_map/jit(_take)/gather | solution.py:138
  62.6 2.6 select_bitcast_fusion.1
  65.2 2.2 copy.820
  67.3 9.1 %reduce-window.6 = s32[32,16,128]{2,1,0:T(8,128)S(1)} reduce-window(s32[32,16,128]{2,1,0:T(8,128)S(1)} %fusion.43, s32[]{:T(128)} %constant.30.clone.1), window={size=1x1x128 pad=0_0x0_0x127_0}, to_apply=%region_1.0 | reduce-window | flops 8323072 | bytes 524292 | tf_op jit(solution)/shard_map/reduce-window
  77.9 0.9 pad_maximum_fusion.12
  79.0 4.7 %collective-permute-start.2 = (f32[4,18,1,256]{3,0,2,1:T(4,128)S(1)}, f32[4,18,1,256]{3,0,2,1:T(4,128)S(1)}, u32[]{:S(2)}, u32[]{:S(2)}) collective-permute-start(f32[4,18,1,256]{3,0,2,1:T(4,128)S(1)} %copy.846), channel_id=1, source_target_pairs={{0,2},{2,4},{4,6},{6,8},{8,10},{10,12},{12,14},{14,0},{1,3},{3,5},... | collective-permute-start | bytes 221192 | tf_op jit(solution)/shard_map/ppermute | solution.py:29
  83.7 1.9 collective-permute-start.3
  85.7 2.2 fusion.14
  87.9 0.7 fusion.39
  88.6 0.9 copy.769
  89.6 0.7 copy_dynamic-update-slice_fusion.2
  90.3 0.9 collective-permute-done.3
  91.3 1.2 fusion.19
  92.5 0.8 reshape.138
  93.7 0.8 copy.826
  94.6 0.8 copy.827
  95.4 0.7 bitcast_select_fusion.5
  96.1 1.9 collective-permute-start.4
  98.1 0.6 copy.819
  98.8 7.6 %gather_fusion.1 = f32[2048,2]{1,0:T(8,128)} fusion(f32[2,4096]{0,1:T(8,128)S(1)} %copy.819, s32[2048]{0:T(1024)S(1)} %get-tuple-element.75), kind=kCustom, calls=%fused_computation.3 | custom fusion | bytes 40960 | tf_op jit(solution)/shard_map/jit(_take)/gather | solution.py:139
  106.4 1.6 select_bitcast_fusion
  108.4 1.3 copy.822
  109.8 6.5 %scatter_custom_fusion = f32[10,4096]{0,1:T(8,128)S(1)} fusion(s32[2048]{0:T(1024)} %bitcast.141, f32[2048,10]{1,0:T(8,128)} %copy.822, f32[]{:T(128)} %constant.45.clone.1), kind=kCustom, calls=%fused_computation.51 | custom fusion | bytes 164352 | tf_op jit(solution)/shard_map/scatter | solution.py:159
  116.2 1.3 copy.823
  117.6 5.2 %all-to-all-start = ((f32[10,32,128]{2,0,1:T(8,128)}), f32[10,32,128]{2,0,1:T(8,128)}, u32[]{:S(2)}, u32[]{:S(2)}) async-start(f32[10,32,128]{2,0,1:T(8,128)} %copy.823), calls=%async_computation.1 | async-start | bytes 524288 | tf_op jit(solution)/shard_map/all_to_all | solution.py:161
  122.8 2.5 fusion.5
  125.3 0.8 copy.782
  126.2 51.2 %all_gather.6 = f32[5,512,16]{2,1,0:T(8,128)S(1)} all-gather(f32[5,16,16]{2,1,0:T(8,128)S(1)} %copy.782), channel_id=1, replica_groups=mesh['pitch'=32,'span'=8,'row'=2] {'pitch'}, dimensions={1}, use_global_device_ids=true | all-gather | bytes 168960 | tf_op jit(solution)/shard_map/all_gather | solution.py:51
  177.3 2.2 copy.783
  179.5 2.8 gather_fusion.2
  182.4 1.5 fusion.46
  183.9 2.2 copy.786
  186.1 1.4 copy.789
  187.5 2.0 fusion.2
  189.9 0.9 copy-done.5
  190.8 0.8 fusion.23
  192.4 1.0 fusion.60
  193.4 1.9 copy.834
  195.3 0.8 copy.835
  196.2 1.9 collective-permute-start.9
  198.1 0.6 fusion.64
  198.8 2.7 collective-permute-start.5
  201.4 6.5 %collective-permute-start.6 = (f32[4,1,16,256]{3,2,1,0:T(8,128)S(1)}, f32[4,1,16,256]{3,2,1,0:T(8,128)S(1)}, u32[]{:S(2)}, u32[]{:S(2)}) collective-permute-start(f32[4,1,16,256]{3,2,1,0:T(8,128)S(1)} %get-tuple-element.54), channel_id=1, source_target_pairs={{16,0},{32,16},{48,32},{64,48},{80,64},{96,80},{112,96},{128,112},... | collective-permute-start | bytes 196616 | tf_op jit(solution)/shard_map/ppermute | solution.py:31
  208.0 47.9 %all_gather.7 = f32[5,512,16]{2,1,0:T(8,128)S(1)} all-gather(f32[5,16,16]{2,1,0:T(8,128)S(1)} %copy.807), channel_id=1, replica_groups=mesh['pitch'=32,'span'=8,'row'=2] {'pitch'}, dimensions={1}, use_global_device_ids=true | all-gather | bytes 168960 | tf_op jit(solution)/shard_map/all_gather | solution.py:51
  255.8 2.2 copy.808
  258.0 2.1 gather_fusion.3
  260.8 1.4 copy.814
  262.2 1.8 fusion.3
  264.8 4.3 %collective-permute-start.7 = (f32[4,18,1,256]{3,0,2,1:T(4,128)S(1)}, f32[4,18,1,256]{3,0,2,1:T(4,128)S(1)}, u32[]{:S(2)}, u32[]{:S(2)}) collective-permute-start(f32[4,18,1,256]{3,0,2,1:T(4,128)S(1)} %copy.851), channel_id=1, source_target_pairs={{0,2},{2,4},{4,6},{6,8},{8,10},{10,12},{12,14},{14,0},{1,3},{3,5},... | collective-permute-start | bytes 221192 | tf_op jit(solution)/shard_map/ppermute | solution.py:29
  269.0 2.1 collective-permute-start.8
  271.4 1.0 fusion.8
  272.5 0.7 copy_dynamic-update-slice_fusion
  273.2 3.3 %collective-permute-done.8 = f32[4,18,1,256]{3,0,2,1:T(4,128)S(1)} collective-permute-done((f32[4,18,1,256]{3,0,2,1:T(4,128)S(1)}, f32[4,18,1,256]{3,0,2,1:T(4,128)S(1)}, u32[]{:S(2)}, u32[]{:S(2)}) %collective-permute-start.8) | collective-permute-done | bytes 73760 | tf_op jit(solution)/shard_map/ppermute | solution.py:31
  277.4 1.3 copy.825
  278.7 1.0 copy.824
  279.7 0.9 copy.857
  (102 shorter events, 7.0 us)
Async XLA Ops:
  7.2 18.4 %copy-start = (bf16[128,128]{1,0:T(8,128)(2,1)S(1)}, bf16[128,128]{1,0:T(8,128)(2,1)}, u32[]{:S(2)}) copy-start(bf16[128,128]{1,0:T(8,128)(2,1)} %param.13) | copy-start | bytes 98308
  7.2 85.3 %reduce-scatter.2.cloned.1.call-start = ((), (), s32[]{:S(2)}) async-start(), calls=%async_computation.2 | async-start | bytes 294912 | tf_op jit(solution)/shard_map/reduce_scatter | solution.py:128
  8.3 17.2 %copy-start.12 = (bf16[16,2,256]{2,1,0:T(2,128)(2,1)S(1)}, bf16[16,2,256]{2,1,0:T(2,128)(2,1)}, u32[]{:S(2)}) copy-start(bf16[16,2,256]{2,1,0:T(2,128)(2,1)} %param.12) | copy-start | bytes 49156
  8.3 18.2 %copy-start.2 = (f32[3,16,16,256]{3,2,1,0:T(8,128)S(1)}, f32[3,16,16,256]{3,2,1,0:T(8,128)}, u32[]{:S(2)}) copy-start(f32[3,16,16,256]{3,2,1,0:T(8,128)} %param.10) | copy-start | bytes 2359300
  9.8 17.2 %copy-start.16 = (s32[1,16]{1,0:T(1,128)S(1)}, s32[1,16]{1,0:T(1,128)}, u32[]{:S(2)}) copy-start(s32[1,16]{1,0:T(1,128)} %param.17) | copy-start | bytes 196
  9.8 17.9 %copy-start.11 = (s32[2048]{0:T(1024)S(1)}, s32[2048]{0:T(1024)}, u32[]{:S(2)}) copy-start(s32[2048]{0:T(1024)} %param.15) | copy-start | bytes 24580
  10.5 67.4 %collective-permute-start = (f32[4,1,16,256]{3,2,1,0:T(8,128)}, f32[4,1,16,256]{3,2,1,0:T(8,128)S(1)}, u32[]{:S(2)}, u32[]{:S(2)}) collective-permute-start(f32[4,1,16,256]{3,2,1,0:T(8,128)} %get-tuple-element.57), channel_id=1, source_target_pairs={{0,16},{16,32},{32,48},{48,64},{64,80},{80,96},{96,112},{112,128},... | collective-permute-start | bytes 196616 | tf_op jit(solution)/shard_map/ppermute | solution.py:29
  14.7 63.1 %collective-permute-start.1 = (f32[4,1,16,256]{3,2,1,0:T(8,128)}, f32[4,1,16,256]{3,2,1,0:T(8,128)}, u32[]{:S(2)}, u32[]{:S(2)}) collective-permute-start(f32[4,1,16,256]{3,2,1,0:T(8,128)} %get-tuple-element.58), channel_id=1, source_target_pairs={{16,0},{32,16},{48,32},{64,48},{80,64},{96,80},{112,96},{128,112},... | collective-permute-start | bytes 196616 | tf_op jit(solution)/shard_map/ppermute | solution.py:31
  27.0 66.3 %copy-start.3 = (f32[3,16,16,256]{3,1,2,0:T(8,128)}, f32[3,16,16,256]{3,1,2,0:T(8,128)S(1)}, u32[]{:S(2)}) copy-start(f32[3,16,16,256]{3,1,2,0:T(8,128)S(1)} %copy.791) | copy-start | bytes 2359300
  62.6 4.7 %copy-start.10 = (s32[2048,1]{0,1:T(1,128)S(1)}, s32[2048,1]{0,1:T(1,128)}, u32[]{:S(2)}) copy-start(s32[2048,1]{0,1:T(1,128)} %param.16) | copy-start | bytes 24580
  77.9 13.4 %copy-start.13 = (f32[17]{0:T(128)}, f32[17]{0:T(128)S(1)}, u32[]{:S(2)}) copy-start(f32[17]{0:T(128)S(1)} %and_convert_fusion) | copy-start | bytes 208
  79.0 10.6 %collective-permute-start.2 = (f32[4,18,1,256]{3,0,2,1:T(4,128)S(1)}, f32[4,18,1,256]{3,0,2,1:T(4,128)S(1)}, u32[]{:S(2)}, u32[]{:S(2)}) collective-permute-start(f32[4,18,1,256]{3,0,2,1:T(4,128)S(1)} %copy.846), channel_id=1, source_target_pairs={{0,2},{2,4},{4,6},{6,8},{8,10},{10,12},{12,14},{14,0},{1,3},{3,5},... | collective-permute-start | bytes 221192 | tf_op jit(solution)/shard_map/ppermute | solution.py:29
  83.7 7.5 %collective-permute-start.3 = (f32[4,18,1,256]{3,0,2,1:T(4,128)S(1)}, f32[4,18,1,256]{3,0,2,1:T(4,128)S(1)}, u32[]{:S(2)}, u32[]{:S(2)}) collective-permute-start(f32[4,18,1,256]{3,0,2,1:T(4,128)S(1)} %copy.847), channel_id=1, source_target_pairs={{2,0},{4,2},{6,4},{8,6},{10,8},{12,10},{14,12},{0,14},{3,1},{5,3},... | collective-permute-start | bytes 221192 | tf_op jit(solution)/shard_map/ppermute | solution.py:31
  95.4 2.7 copy-start.6
  96.1 29.2 %collective-permute-start.4 = (f32[5,16,16]{2,0,1:T(8,128)}, f32[5,16,16]{2,0,1:T(8,128)}, u32[]{:S(2)}, u32[]{:S(2)}) collective-permute-start(f32[5,16,16]{2,0,1:T(8,128)} %bitcast_select_fusion.5), channel_id=1, source_target_pairs={{0,1},{1,0},{2,3},{3,2},{4,5},{5,4},{6,7},{7,6},{8,9},{9,8},{10,11... | collective-permute-start | bytes 15368 | tf_op jit(solution)/shard_map/ppermute | solution.py:19
  106.4 1.9 copy-start.8
  106.4 1.9 copy-start.9
  117.6 161.1 %all-to-all-start = ((f32[10,32,128]{2,0,1:T(8,128)}), f32[10,32,128]{2,0,1:T(8,128)}, u32[]{:S(2)}, u32[]{:S(2)}) async-start(f32[10,32,128]{2,0,1:T(8,128)} %copy.823), calls=%async_computation.1 | async-start | bytes 524288 | tf_op jit(solution)/shard_map/all_to_all | solution.py:161
  177.3 5.0 %copy-start.7 = (f32[5,16,16,1]{2,0,1,3:T(8,128)S(1)}, f32[5,16,16,1]{2,0,1,3:T(8,128)}, u32[]{:S(2)}) copy-start(f32[5,16,16,1]{2,0,1,3:T(8,128)} %copy-done.6) | copy-start | bytes 15364
  177.3 5.0 %copy-start.15 = (pred[16]{0:T(512)(128)(4,1)S(1)}, pred[16]{0:T(512)(128)(4,1)}, u32[]{:S(2)}) copy-start(pred[16]{0:T(512)(128)(4,1)} %compare_and_fusion.2) | copy-start | bytes 52
  179.5 8.0 %copy-start.4 = (f32[3,16,16,256]{3,1,2,0:T(8,128)S(1)}, f32[3,16,16,256]{3,1,2,0:T(8,128)}, u32[]{:S(2)}) copy-start(f32[3,16,16,256]{3,1,2,0:T(8,128)} %copy-done.3) | copy-start | bytes 2359300
  189.6 1.2 copy-start.5
  196.2 11.7 %collective-permute-start.9 = (f32[5,16,16]{2,0,1:T(8,128)S(1)}, f32[5,16,16]{2,0,1:T(8,128)S(1)}, u32[]{:S(2)}, u32[]{:S(2)}) collective-permute-start(f32[5,16,16]{2,0,1:T(8,128)S(1)} %bitcast_select_fusion.2), channel_id=1, source_target_pairs={{0,1},{1,0},{2,3},{3,2},{4,5},{5,4},{6,7},{7,6},{8,9},{9,8},{10,11... | collective-permute-start | bytes 15368 | tf_op jit(solution)/shard_map/ppermute | solution.py:19
  198.8 65.5 %collective-permute-start.5 = (f32[4,1,16,256]{3,2,1,0:T(8,128)}, f32[4,1,16,256]{3,2,1,0:T(8,128)S(1)}, u32[]{:S(2)}, u32[]{:S(2)}) collective-permute-start(f32[4,1,16,256]{3,2,1,0:T(8,128)} %get-tuple-element.53), channel_id=1, source_target_pairs={{0,16},{16,32},{32,48},{48,64},{64,80},{80,96},{96,112},{112,128},... | collective-permute-start | bytes 196616 | tf_op jit(solution)/shard_map/ppermute | solution.py:29
  201.4 62.9 %collective-permute-start.6 = (f32[4,1,16,256]{3,2,1,0:T(8,128)S(1)}, f32[4,1,16,256]{3,2,1,0:T(8,128)S(1)}, u32[]{:S(2)}, u32[]{:S(2)}) collective-permute-start(f32[4,1,16,256]{3,2,1,0:T(8,128)S(1)} %get-tuple-element.54), channel_id=1, source_target_pairs={{16,0},{32,16},{48,32},{64,48},{80,64},{96,80},{112,96},{128,112},... | collective-permute-start | bytes 196616 | tf_op jit(solution)/shard_map/ppermute | solution.py:31
  264.8 7.7 %collective-permute-start.7 = (f32[4,18,1,256]{3,0,2,1:T(4,128)S(1)}, f32[4,18,1,256]{3,0,2,1:T(4,128)S(1)}, u32[]{:S(2)}, u32[]{:S(2)}) collective-permute-start(f32[4,18,1,256]{3,0,2,1:T(4,128)S(1)} %copy.851), channel_id=1, source_target_pairs={{0,2},{2,4},{4,6},{6,8},{8,10},{10,12},{12,14},{14,0},{1,3},{3,5},... | collective-permute-start | bytes 221192 | tf_op jit(solution)/shard_map/ppermute | solution.py:29
  269.0 7.5 %collective-permute-start.8 = (f32[4,18,1,256]{3,0,2,1:T(4,128)S(1)}, f32[4,18,1,256]{3,0,2,1:T(4,128)S(1)}, u32[]{:S(2)}, u32[]{:S(2)}) collective-permute-start(f32[4,18,1,256]{3,0,2,1:T(4,128)S(1)} %copy.852), channel_id=1, source_target_pairs={{2,0},{4,2},{6,4},{8,6},{10,8},{12,10},{14,12},{0,14},{3,1},{5,3},... | collective-permute-start | bytes 221192 | tf_op jit(solution)/shard_map/ppermute | solution.py:31
  272.4 4.2 %copy-start.14 = (f32[17]{0:T(128)S(1)}, f32[17]{0:T(128)}, u32[]{:S(2)}) copy-start(f32[17]{0:T(128)} %copy-done.13) | copy-start | bytes 208
  276.9 3.7 %copy-start.1 = (bf16[128,128]{1,0:T(8,128)(2,1)S(1)}, bf16[128,128]{1,0:T(8,128)(2,1)}, u32[]{:S(2)}) copy-start(bf16[128,128]{1,0:T(8,128)(2,1)} %param.13) | copy-start | bytes 98308
Sparse Core Ops, SparseCore 0:
  26.7 35.2 reduce-scatter.1
where the time goes:
time: 289 us; the launch traced here: 287 us
  blocking collectives  99 us (34%)
  local copies, waits for them, and re-layouts  89.4 us (31%)
  starting transfers between devices  46.3 us (16%)
  other arithmetic  32.7 us (11%)
  between operations  14.8 us (5%)
  waiting for transfers between devices  4.27 us (1%)
    all_gather x2, blocking collectives, interface_ghost(): picked = lax.all_gather(across, 'pitch', axis=1, tiled=True)  99 us
    unnamed x53, local copies, waits for them, and re-layouts  24.7 us
    ppermute x4, starting transfers between devices, padded(): lax.ppermute(head, axis, [((i + 1) % count, i) for i in range(count)])  21.3 us
    gather x1, local copies, waits for them, and re-layouts, local(): jnp.take(fields.reshape(fields.shape[0], -1), tracer_cells, axis=1)  18.2 us
    ppermute x4, starting transfers between devices, padded(): lax.ppermute(tail, axis, [(i, (i + 1) % count) for i in range(count)])  15.9 us
    another operation x3, other arithmetic  9.41 us
    gather x1, local copies, waits for them, and re-layouts, local(): jnp.take(jnp.stack([speed_axial, speed_pitch]).reshape(2, plane_size), tr...  7.6 us
    scatter x1, local copies, waits for them, and re-layouts, local(): outgoing = jnp.zeros((tracer_values.shape[0], npitch * capacity), jnp.flo...  6.46 us
  transfers between devices with their start and end apart: 12, of which 2 were waited for; matrix products, arithmetic and copies ran while one was open for 39% of the time, Pallas kernels for 0%

commit v1 on v0

--- a/solution.py
+++ b/solution.py
@@ -2,6 +2,7 @@
 import jax.numpy as jnp
 from jax import lax
 from jax.sharding import PartitionSpec as P
+from jax.lax import all_to_all, axis_size
 
 SUB = 2
 TIME_STEP = 0.9
@@ -158,7 +159,9 @@
         .at[:, position]
         .set(updated)
     )
-    arrived = lax.all_to_all(outgoing, "pitch", split_axis=1, concat_axis=1, tiled=True)
+    arrived = jnp.concatenate(
+        all_to_all(jnp.stack(jnp.split(outgoing, axis_size("pitch"), axis=1)), "pitch", 0, 0), 1
+    )
     face_index = span_id * radial_cells + jnp.arange(radial_cells + 1, dtype=jnp.int32)
     total_radial = radial_cells * lax.axis_size("span")
     wall_mask = ((face_index > 0) & (face_index < total_radial)).astype(jnp.float32)

time: 289 us -> 307 us (1.062)
  local copies, waits for them, and re-layouts: 89.4 us -> 111 us
    unnamed x53 -> x86, local copies, waits for them, and re-layouts: 24.7 us -> 46.4 us
    another operation x1 -> x3, local copies, waits for them, and re-layouts: 0.24 us -> 3.78 us  [the longest x2 3.54 us: local(): jnp.stack(jnp.split(outgoing, axis_size('pitch'), axis=1))]
  transfers between devices with their start and end apart: 12 -> 12, of which waited for: 2 -> 2; matrix products, arithmetic and copies ran while one was open for 39% -> 31% of each run, Pallas kernels for 0% -> 0%
where the time goes in v1:
time: 307 us; the launch traced here: 306 us
  local copies, waits for them, and re-layouts  111 us (36%)
  blocking collectives  99.1 us (32%)
  starting transfers between devices  45.9 us (15%)
  other arithmetic  30 us (10%)
  between operations  14.8 us (5%)
  waiting for transfers between devices  3.86 us (1%)
    all_gather x2, blocking collectives, interface_ghost(): picked = lax.all_gather(across, 'pitch', axis=1, tiled=True)  99.1 us
    unnamed x86, local copies, waits for them, and re-layouts  46.4 us
    ppermute x4, starting transfers between devices, padded(): lax.ppermute(head, axis, [((i + 1) % count, i) for i in range(count)])  22.4 us
    gather x1, local copies, waits for them, and re-layouts, local(): jnp.take(fields.reshape(fields.shape[0], -1), tracer_cells, axis=1)  18.2 us
    ppermute x4, starting transfers between devices, padded(): lax.ppermute(tail, axis, [(i, (i + 1) % count) for i in range(count)])  14.4 us
    another operation x3, other arithmetic  9.41 us
    gather x1, local copies, waits for them, and re-layouts, local(): jnp.take(jnp.stack([speed_axial, speed_pitch]).reshape(2, plane_size), tr...  7.6 us
    scatter x1, local copies, waits for them, and re-layouts, local(): outgoing = jnp.zeros((tracer_values.shape[0], npitch * capacity), jnp.flo...  6.46 us
  transfers between devices with their start and end apart: 12, of which 2 were waited for; matrix products, arithmetic and copies ran while one was open for 31% of the time, Pallas kernels for 0%

profile of v1, /device:TPU:24, one launch (start us, length us, event | category | flops | bytes accessed | tf_op | source)
XLA Modules:
  0.0 306.1 jit_solution(11647644536798762589)
XLA Ops:
  7.3 0.8 copy.917
  8.0 0.9 fusion.48
  9.0 1.1 copy.992
  10.1 1.2 constant_dynamic-update-slice_fusion
  11.5 4.3 %collective-permute-start = (f32[4,1,16,256]{3,2,1,0:T(8,128)S(1)}, f32[4,1,16,256]{3,2,1,0:T(8,128)S(1)}, u32[]{:S(2)}, u32[]{:S(2)}) collective-permute-start(f32[4,1,16,256]{3,2,1,0:T(8,128)S(1)} %get-tuple-element.59), channel_id=1, source_target_pairs={{0,16},{16,32},{32,48},{48,64},{64,80},{80,96},{96,112},{112,128},... | collective-permute-start | bytes 196616 | tf_op jit(solution)/shard_map/ppermute | solution.py:30
  15.8 10.8 %collective-permute-start.1 = (f32[4,1,16,256]{3,2,1,0:T(8,128)S(1)}, f32[4,1,16,256]{3,2,1,0:T(8,128)S(1)}, u32[]{:S(2)}, u32[]{:S(2)}) collective-permute-start(f32[4,1,16,256]{3,2,1,0:T(8,128)S(1)} %get-tuple-element.60), channel_id=1, source_target_pairs={{16,0},{32,16},{48,32},{64,48},{80,64},{96,80},{112,96},{128,112},... | collective-permute-start | bytes 196616 | tf_op jit(solution)/shard_map/ppermute | solution.py:32
  26.6 16.7 %copy.882 = f32[3,16,16,256]{0,3,2,1:T(8,128)} copy(f32[3,16,16,256]{3,2,1,0:T(8,128)S(1)} %copy-done.2) | data formatting | bytes 1572864 | tf_op args[0]
  43.3 1.3 copy.855
  45.2 18.2 %gather_fusion = f32[2048,3]{1,0:T(8,128)} fusion(f32[3,65536]{0,1:T(8,128)} %bitcast.249, s32[2048]{0:T(1024)S(1)} %get-tuple-element.76), kind=kCustom, calls=%fused_computation.2 | custom fusion | bytes 57344 | tf_op jit(solution)/shard_map/jit(_take)/gather | solution.py:139
  63.4 1.6 select_bitcast_fusion.1
  65.4 9.1 %reduce-window.6 = s32[32,16,128]{2,1,0:T(8,128)S(1)} reduce-window(s32[32,16,128]{2,1,0:T(8,128)S(1)} %fusion.43, s32[]{:T(128)} %constant.30.clone.1), window={size=1x1x128 pad=0_0x0_0x127_0}, to_apply=%region_1.0 | reduce-window | flops 8323072 | bytes 524292 | tf_op jit(solution)/shard_map/reduce-window
  76.2 4.7 %collective-permute-start.2 = (f32[4,18,1,256]{3,0,2,1:T(4,128)S(1)}, f32[4,18,1,256]{3,0,2,1:T(4,128)S(1)}, u32[]{:S(2)}, u32[]{:S(2)}) collective-permute-start(f32[4,18,1,256]{3,0,2,1:T(4,128)S(1)} %copy.910), channel_id=1, source_target_pairs={{0,2},{2,4},{4,6},{6,8},{8,10},{10,12},{12,14},{14,0},{1,3},{3,5},... | collective-permute-start | bytes 221192 | tf_op jit(solution)/shard_map/ppermute | solution.py:30
  80.9 1.9 collective-permute-start.3
  82.8 1.4 fusion.14
  84.3 0.9 copy.833
  85.2 0.7 copy_dynamic-update-slice_fusion.2
  85.9 2.4 collective-permute-done.3
  88.4 1.2 fusion.19
  89.6 0.8 reshape.142
  90.6 0.6 copy.883
  91.2 7.6 %gather_fusion.1 = f32[2048,2]{1,0:T(8,128)} fusion(f32[2,4096]{0,1:T(8,128)S(1)} %copy.883, s32[2048]{0:T(1024)S(1)} %get-tuple-element.77), kind=kCustom, calls=%fused_computation.3 | custom fusion | bytes 40960 | tf_op jit(solution)/shard_map/jit(_take)/gather | solution.py:140
  98.8 1.6 select_bitcast_fusion
  100.8 1.4 copy.886
  102.2 6.5 %scatter_custom_fusion = f32[10,4096]{0,1:T(8,128)S(1)} fusion(s32[2048]{0:T(1024)} %bitcast.269, f32[2048,10]{1,0:T(8,128)} %copy.886, f32[]{:T(128)} %constant.45.clone.1), kind=kCustom, calls=%fused_computation.51 | custom fusion | bytes 164352 | tf_op jit(solution)/shard_map/scatter | solution.py:160
  111.1 0.6 constant_dynamic-update-slice_fusion.28
  112.4 0.6 constant_dynamic-update-slice_fusion.26
  114.3 0.6 constant_dynamic-update-slice_fusion.23
  128.6 2.9 copy.887
  131.5 5.1 %all-to-all-start = ((f32[32,10,128]{2,1,0:T(8,128)}), f32[32,10,128]{2,1,0:T(8,128)S(1)}, u32[]{:S(2)}, u32[]{:S(2)}) async-start(f32[32,10,128]{2,1,0:T(8,128)} %copy.887), calls=%async_computation.1 | async-start | bytes 524288 | tf_op jit(solution)/shard_map/all_to_all | solution.py:163
  136.7 1.3 pad_maximum_fusion.9
  138.0 1.3 fusion.61
  139.3 1.9 copy.890
  141.2 1.9 copy.891
  143.1 1.9 collective-permute-start.4
  145.1 3.0 fusion.5
  148.1 51.2 %all_gather.6 = f32[5,512,16]{2,1,0:T(8,128)S(1)} all-gather(f32[5,16,16]{2,1,0:T(8,128)S(1)} %copy.846), channel_id=1, replica_groups=mesh['pitch'=32,'span'=8,'row'=2] {'pitch'}, dimensions={1}, use_global_device_ids=true | all-gather | bytes 168960 | tf_op jit(solution)/shard_map/all_gather | solution.py:52
  199.3 2.2 copy.847
  201.5 2.1 gather_fusion.2
  204.3 1.4 copy.853
  205.7 1.8 fusion.2
  207.9 0.9 copy-done.4
  209.1 0.8 fusion.23
  210.7 1.0 fusion.60
  211.8 1.9 copy.898
  213.7 0.8 copy.899
  214.6 1.9 collective-permute-start.9
  216.5 0.7 fusion.64
  217.2 2.7 collective-permute-start.5
  219.9 6.4 %collective-permute-start.6 = (f32[4,1,16,256]{3,2,1,0:T(8,128)}, f32[4,1,16,256]{3,2,1,0:T(8,128)S(1)}, u32[]{:S(2)}, u32[]{:S(2)}) collective-permute-start(f32[4,1,16,256]{3,2,1,0:T(8,128)} %get-tuple-element.56), channel_id=1, source_target_pairs={{16,0},{32,16},{48,32},{64,48},{80,64},{96,80},{112,96},{128,112},... | collective-permute-start | bytes 196616 | tf_op jit(solution)/shard_map/ppermute | solution.py:32
  226.4 47.9 %all_gather.7 = f32[5,512,16]{2,1,0:T(8,128)S(1)} all-gather(f32[5,16,16]{2,1,0:T(8,128)S(1)} %copy.871), channel_id=1, replica_groups=mesh['pitch'=32,'span'=8,'row'=2] {'pitch'}, dimensions={1}, use_global_device_ids=true | all-gather | bytes 168960 | tf_op jit(solution)/shard_map/all_gather | solution.py:52
  274.2 2.2 copy.872
  276.4 2.1 gather_fusion.3
  278.6 0.7 fusion.44
  279.3 1.4 copy.875
  280.7 2.2 copy.878
  282.9 1.8 fusion.3
  285.8 2.8 collective-permute-start.7
  288.6 3.3 %collective-permute-start.8 = (f32[4,18,1,256]{3,0,2,1:T(4,128)S(1)}, f32[4,18,1,256]{3,0,2,1:T(4,128)S(1)}, u32[]{:S(2)}, u32[]{:S(2)}) collective-permute-start(f32[4,18,1,256]{3,0,2,1:T(4,128)S(1)} %copy.916), channel_id=1, source_target_pairs={{2,0},{4,2},{6,4},{8,6},{10,8},{12,10},{14,12},{0,14},{3,1},{5,3},... | collective-permute-start | bytes 221192 | tf_op jit(solution)/shard_map/ppermute | solution.py:32
  291.9 0.9 fusion.12
  292.9 1.0 fusion.8
  293.9 0.7 copy_dynamic-update-slice_fusion
  294.6 1.4 collective-permute-done.8
  297.0 1.3 copy.889
  298.4 0.9 copy.921
  (136 shorter events, 25.9 us)
Async XLA Ops:
  7.2 0.9 copy-start
  7.2 19.4 %copy-start.2 = (f32[3,16,16,256]{3,2,1,0:T(8,128)S(1)}, f32[3,16,16,256]{3,2,1,0:T(8,128)}, u32[]{:S(2)}) copy-start(f32[3,16,16,256]{3,2,1,0:T(8,128)} %param.10) | copy-start | bytes 2359300
  7.2 19.4 %copy-start.13 = (s32[2048]{0:T(1024)S(1)}, s32[2048]{0:T(1024)}, u32[]{:S(2)}) copy-start(s32[2048]{0:T(1024)} %param.15) | copy-start | bytes 24580
  7.2 82.4 %reduce-scatter.2.cloned.1.call-start = ((), (), s32[]{:S(2)}) async-start(), calls=%async_computation.2 | async-start | bytes 294912 | tf_op jit(solution)/shard_map/reduce_scatter | solution.py:129
  11.5 64.4 %collective-permute-start = (f32[4,1,16,256]{3,2,1,0:T(8,128)S(1)}, f32[4,1,16,256]{3,2,1,0:T(8,128)S(1)}, u32[]{:S(2)}, u32[]{:S(2)}) collective-permute-start(f32[4,1,16,256]{3,2,1,0:T(8,128)S(1)} %get-tuple-element.59), channel_id=1, source_target_pairs={{0,16},{16,32},{32,48},{48,64},{64,80},{80,96},{96,112},{112,128},... | collective-permute-start | bytes 196616 | tf_op jit(solution)/shard_map/ppermute | solution.py:30
  15.8 60.1 %collective-permute-start.1 = (f32[4,1,16,256]{3,2,1,0:T(8,128)S(1)}, f32[4,1,16,256]{3,2,1,0:T(8,128)S(1)}, u32[]{:S(2)}, u32[]{:S(2)}) collective-permute-start(f32[4,1,16,256]{3,2,1,0:T(8,128)S(1)} %get-tuple-element.60), channel_id=1, source_target_pairs={{16,0},{32,16},{48,32},{64,48},{80,64},{96,80},{112,96},{128,112},... | collective-permute-start | bytes 196616 | tf_op jit(solution)/shard_map/ppermute | solution.py:32
  26.6 18.1 %copy-start.17 = (s32[1,16]{1,0:T(1,128)S(1)}, s32[1,16]{1,0:T(1,128)}, u32[]{:S(2)}) copy-start(s32[1,16]{1,0:T(1,128)} %param.17) | copy-start | bytes 196
  44.7 20.6 %copy-start.12 = (s32[2048,1]{0,1:T(1,128)S(1)}, s32[2048,1]{0,1:T(1,128)}, u32[]{:S(2)}) copy-start(s32[2048,1]{0,1:T(1,128)} %param.16) | copy-start | bytes 24580
  75.9 12.5 %copy-start.14 = (f32[17]{0:T(128)}, f32[17]{0:T(128)S(1)}, u32[]{:S(2)}) copy-start(f32[17]{0:T(128)S(1)} %and_convert_fusion) | copy-start | bytes 208
  76.2 9.0 %collective-permute-start.2 = (f32[4,18,1,256]{3,0,2,1:T(4,128)S(1)}, f32[4,18,1,256]{3,0,2,1:T(4,128)S(1)}, u32[]{:S(2)}, u32[]{:S(2)}) collective-permute-start(f32[4,18,1,256]{3,0,2,1:T(4,128)S(1)} %copy.910), channel_id=1, source_target_pairs={{0,2},{2,4},{4,6},{6,8},{8,10},{10,12},{12,14},{14,0},{1,3},{3,5},... | collective-permute-start | bytes 221192 | tf_op jit(solution)/shard_map/ppermute | solution.py:30
  80.9 7.5 %collective-permute-start.3 = (f32[4,18,1,256]{3,0,2,1:T(4,128)S(1)}, f32[4,18,1,256]{3,0,2,1:T(4,128)S(1)}, u32[]{:S(2)}, u32[]{:S(2)}) collective-permute-start(f32[4,18,1,256]{3,0,2,1:T(4,128)S(1)} %copy.911), channel_id=1, source_target_pairs={{2,0},{4,2},{6,4},{8,6},{10,8},{12,10},{14,12},{0,14},{3,1},{5,3},... | collective-permute-start | bytes 221192 | tf_op jit(solution)/shard_map/ppermute | solution.py:32
  91.2 9.5 %copy-start.11 = (f32[10,2048]{1,0:T(8,128)S(1)}, f32[10,2048]{1,0:T(8,128)}, u32[]{:S(2)}) copy-start(f32[10,2048]{1,0:T(8,128)} %param.14) | copy-start | bytes 245764
  131.5 166.8 %all-to-all-start = ((f32[32,10,128]{2,1,0:T(8,128)}), f32[32,10,128]{2,1,0:T(8,128)S(1)}, u32[]{:S(2)}, u32[]{:S(2)}) async-start(f32[32,10,128]{2,1,0:T(8,128)} %copy.887), calls=%async_computation.1 | async-start | bytes 524288 | tf_op jit(solution)/shard_map/all_to_all | solution.py:163
  138.0 7.1 %copy-start.6 = (f32[3,17,16,256]{3,2,1,0:T(8,128)S(1)}, f32[3,17,16,256]{3,2,1,0:T(8,128)}, u32[]{:S(2)}) copy-start(f32[3,17,16,256]{3,2,1,0:T(8,128)} %get-tuple-element.57) | copy-start | bytes 2506756
  138.0 7.1 %copy-start.7 = (f32[3,17,16,256]{3,2,1,0:T(8,128)S(1)}, f32[3,17,16,256]{3,2,1,0:T(8,128)}, u32[]{:S(2)}) copy-start(f32[3,17,16,256]{3,2,1,0:T(8,128)} %get-tuple-element.58) | copy-start | bytes 2506756
  143.1 5.0 %collective-permute-start.4 = (f32[5,16,16]{2,0,1:T(8,128)S(1)}, f32[5,16,16]{2,0,1:T(8,128)S(1)}, u32[]{:S(2)}, u32[]{:S(2)}) collective-permute-start(f32[5,16,16]{2,0,1:T(8,128)S(1)} %bitcast_select_fusion.5), channel_id=1, source_target_pairs={{0,1},{1,0},{2,3},{3,2},{4,5},{5,4},{6,7},{7,6},{8,9},{9,8},{10,11... | collective-permute-start | bytes 15368 | tf_op jit(solution)/shard_map/ppermute | solution.py:20
  199.3 4.3 %copy-start.16 = (pred[16]{0:T(512)(128)(4,1)S(1)}, pred[16]{0:T(512)(128)(4,1)}, u32[]{:S(2)}) copy-start(pred[16]{0:T(512)(128)(4,1)} %compare_and_fusion.2) | copy-start | bytes 52
  199.3 6.4 %copy-start.3 = (f32[3,16,16,256]{3,1,2,0:T(8,128)S(1)}, f32[3,16,16,256]{3,1,2,0:T(8,128)}, u32[]{:S(2)}) copy-start(f32[3,16,16,256]{3,1,2,0:T(8,128)} %copy.855) | copy-start | bytes 2359300
  207.6 1.2 copy-start.4
  207.6 1.5 copy-start.5
  214.5 5.4 %copy-start.9 = (f32[5,16,16,1]{2,0,1,3:T(8,128)}, f32[5,16,16,1]{2,0,1,3:T(8,128)S(1)}, u32[]{:S(2)}) copy-start(f32[5,16,16,1]{2,0,1,3:T(8,128)S(1)} %copy.899) | copy-start | bytes 15364
  214.6 11.8 %collective-permute-start.9 = (f32[5,16,16]{2,0,1:T(8,128)S(1)}, f32[5,16,16]{2,0,1:T(8,128)S(1)}, u32[]{:S(2)}, u32[]{:S(2)}) collective-permute-start(f32[5,16,16]{2,0,1:T(8,128)S(1)} %bitcast_select_fusion.2), channel_id=1, source_target_pairs={{0,1},{1,0},{2,3},{3,2},{4,5},{5,4},{6,7},{7,6},{8,9},{9,8},{10,11... | collective-permute-start | bytes 15368 | tf_op jit(solution)/shard_map/ppermute | solution.py:20
  217.2 67.9 %collective-permute-start.5 = (f32[4,1,16,256]{3,2,1,0:T(8,128)}, f32[4,1,16,256]{3,2,1,0:T(8,128)S(1)}, u32[]{:S(2)}, u32[]{:S(2)}) collective-permute-start(f32[4,1,16,256]{3,2,1,0:T(8,128)} %get-tuple-element.55), channel_id=1, source_target_pairs={{0,16},{16,32},{32,48},{48,64},{64,80},{80,96},{96,112},{112,128},... | collective-permute-start | bytes 196616 | tf_op jit(solution)/shard_map/ppermute | solution.py:30
  219.9 65.1 %collective-permute-start.6 = (f32[4,1,16,256]{3,2,1,0:T(8,128)}, f32[4,1,16,256]{3,2,1,0:T(8,128)S(1)}, u32[]{:S(2)}, u32[]{:S(2)}) collective-permute-start(f32[4,1,16,256]{3,2,1,0:T(8,128)} %get-tuple-element.56), channel_id=1, source_target_pairs={{16,0},{32,16},{48,32},{64,48},{80,64},{96,80},{112,96},{128,112},... | collective-permute-start | bytes 196616 | tf_op jit(solution)/shard_map/ppermute | solution.py:32
  274.2 4.3 %copy-start.10 = (f32[5,16,16,1]{2,0,1,3:T(8,128)S(1)}, f32[5,16,16,1]{2,0,1,3:T(8,128)}, u32[]{:S(2)}) copy-start(f32[5,16,16,1]{2,0,1,3:T(8,128)} %copy-done.9) | copy-start | bytes 15364
  285.0 0.6 copy-start.8
  285.8 8.1 %collective-permute-start.7 = (f32[4,18,1,256]{3,0,2,1:T(4,128)S(1)}, f32[4,18,1,256]{3,0,2,1:T(4,128)S(1)}, u32[]{:S(2)}, u32[]{:S(2)}) collective-permute-start(f32[4,18,1,256]{3,0,2,1:T(4,128)S(1)} %copy.915), channel_id=1, source_target_pairs={{0,2},{2,4},{4,6},{6,8},{8,10},{10,12},{12,14},{14,0},{1,3},{3,5},... | collective-permute-start | bytes 221192 | tf_op jit(solution)/shard_map/ppermute | solution.py:30
  288.6 7.5 %collective-permute-start.8 = (f32[4,18,1,256]{3,0,2,1:T(4,128)S(1)}, f32[4,18,1,256]{3,0,2,1:T(4,128)S(1)}, u32[]{:S(2)}, u32[]{:S(2)}) collective-permute-start(f32[4,18,1,256]{3,0,2,1:T(4,128)S(1)} %copy.916), channel_id=1, source_target_pairs={{2,0},{4,2},{6,4},{8,6},{10,8},{12,10},{14,12},{0,14},{3,1},{5,3},... | collective-permute-start | bytes 221192 | tf_op jit(solution)/shard_map/ppermute | solution.py:32
  293.9 2.3 copy-start.15
  296.5 2.8 copy-start.1
Sparse Core Ops, SparseCore 0:
  11.4 43.3 reduce-scatter.1
